TPU v7x, 32 devices: a whole 2x2x4 slice. The times are simulated.
32 devices in a mesh: heads: 4 (over y, x), fsdp: 8 (over z, core).
Axes of the slice: x: 2, y: 2, z: 4, core: 2. Of those that a mesh axis runs over, the one named last changes fastest.
Arguments:
- inputs: bfloat16 [8, 3072, 1280], P('fsdp', 'heads'), may hold values from -6 to 6
- cotangent: bfloat16 [8, 3072, 1280], P('fsdp', 'heads'), may hold values from -6 to 6
- lengths: int32 [8, 3], P('fsdp'), may hold values from 1 to 1024, 1536 in all within a row
- adapter_ids: int32 [8, 4], P('fsdp'), may hold values from 0 to 7
- query_weight: bfloat16 [1280, 1280], P('fsdp'), may hold values from -0.15625 to 0.15625
- key_weight: bfloat16 [1280, 1280], P('fsdp'), may hold values from -0.15625 to 0.15625
- value_weight: bfloat16 [1280, 1280], P('fsdp'), may hold values from -0.15625 to 0.15625
- out_weight: bfloat16 [1280, 1280], P('fsdp'), may hold values from -1.25 to 1.25
- up_weight: bfloat16 [1280, 1280], P('fsdp'), may hold values from -0.15625 to 0.15625
- down_weight: bfloat16 [1280, 1280], P('fsdp'), may hold values from -0.15625 to 0.15625
- attn_gain: bfloat16 [1280], replicated, may hold values from 0.099609375 to 1.8984375
- mlp_gain: bfloat16 [1280], replicated, may hold values from 0.099609375 to 1.8984375
- query_scale: float32 [80], replicated, may hold values from 0.5 to 2
- adapter_in: bfloat16 [4, 8, 1280, 16], replicated, may hold values from -0.15625 to 0.15625
- adapter_out: bfloat16 [4, 8, 16, 1280], replicated, may hold values from -1.5 to 1.5
Outputs:
- outputs: bfloat16 [8, 3072, 1280], P('fsdp', 'heads')
- grad_inputs: float32 [8, 3072, 1280], P('fsdp', 'heads')
- grad_adapter_in: float32 [4, 8, 1280, 16], replicated
- grad_adapter_out: float32 [4, 8, 16, 1280], replicated
Inputs may be any that keep to these rules, and one draw needn't show every extreme that they name: In every group the 3 lengths sum to 1536, and the longest is 1024.
All inputs are finite; a program needn't handle non-finite values.
Results may differ from a plain program's by a relative error of at most 0.015.
The roundings to bfloat16 on the way count: a program that leaves them out, or rounds other values in their place, can miss the bound.
Values may be sent and summed in bfloat16 or wider, within the bound.
No kernel may reach another device: no remote copies, remote signals or barrier semaphores. Data moves between devices by JAX's collectives and lax.ppermute only.
A program may use at most 256 MiB of HBM per device.

v0:
```python
import jax
import jax.numpy as jnp
from jax import lax
from jax.sharding import PartitionSpec as P

D = 1280
HEADS = 16
HEAD_DIM = 80
RANK = 16
ADAPTERS = 8
CONTS = 3
CONT_LEN = 512
PROMPT_LEN = 1536
GROUP_TOK = 3072
EPSILON = 1e-06


def product(left, right):
    return jnp.dot(left, right, preferred_element_type=jnp.float32)


def contract_rows(left, right):
    return lax.dot_general(
        left, right, (((0,), (0,)), ((), ())), preferred_element_type=jnp.float32
    )


def contract_cols(left, right):
    return lax.dot_general(
        left, right, (((1,), (1,)), ((), ())), preferred_element_type=jnp.float32
    )


def normalize(values, gain_vec):
    scaling = lax.rsqrt(jnp.mean(values * values, axis=-1, keepdims=True) + EPSILON)
    return (values * scaling * gain_vec, scaling)


def normalize_back(values, scaling, gain_vec, upstream):
    weighted = gain_vec * upstream
    return scaling * weighted - values * scaling**3 * jnp.mean(
        values * weighted, axis=-1, keepdims=True
    )


def segment_of(length_row):
    places = jnp.arange(GROUP_TOK, dtype=jnp.int32)
    bounds = jnp.cumsum(length_row)
    passed = jnp.sum((places[:, None] - PROMPT_LEN >= bounds[None, :]).astype(jnp.int32), axis=1)
    return jnp.where(places < PROMPT_LEN, 0, 1 + passed)


def picker(segments, id_row):
    member = (segments[:, None] == jnp.arange(CONTS + 1, dtype=jnp.int32)[None, :]).astype(
        jnp.int32
    )
    token_ids = jnp.sum(member * id_row[None, :], axis=1)
    columns = jnp.arange(ADAPTERS * RANK, dtype=jnp.int32) // RANK
    return (token_ids[:, None] == columns[None, :]).astype(jnp.float32)


def adapter_forward(normed_low, flat_down, flat_up, chosen):
    inner_low = (product(normed_low, flat_down) * chosen).astype(jnp.bfloat16)
    return (inner_low, product(inner_low, flat_up))


def adapter_backward(normed_low, inner_low, upstream_low, flat_down, flat_up, chosen):
    grad_up = contract_rows(inner_low, upstream_low)
    spread = (contract_cols(upstream_low, flat_up) * chosen).astype(jnp.bfloat16)
    grad_down = contract_rows(normed_low, spread)
    return (grad_down, grad_up, contract_cols(spread, flat_down))


def block_masks(segments):
    places = jnp.arange(GROUP_TOK, dtype=jnp.int32)
    block_count = GROUP_TOK // CONT_LEN
    return (
        places,
        segments == 0,
        places.reshape(block_count, CONT_LEN),
        segments.reshape(block_count, CONT_LEN),
    )


def attend_forward(query_heads, key_heads, value_heads, segments):
    block_count = GROUP_TOK // CONT_LEN
    width_here = query_heads.shape[1]
    heads_here = width_here // HEAD_DIM
    key_split = key_heads.reshape(GROUP_TOK, heads_here, HEAD_DIM)
    value_split = value_heads.reshape(GROUP_TOK, heads_here, HEAD_DIM)
    places, prompt_col, row_place_blocks, row_segment_blocks = block_masks(segments)

    def one_block(pieces):
        query_block, row_places, row_segments = pieces
        scores = jnp.einsum(
            "qhd,khd->hqk", query_block, key_split, preferred_element_type=jnp.float32
        )
        allowed = (places[None, :] <= row_places[:, None]) & (
            prompt_col[None, :] | (segments[None, :] == row_segments[:, None])
        )
        scores = jnp.where(allowed[None], scores, -1e30)
        largest = jnp.max(scores, axis=-1, keepdims=True)
        exponent = jnp.exp(scores - largest)
        row_total = jnp.sum(exponent, axis=-1, keepdims=True)
        probability = (exponent / row_total).astype(jnp.bfloat16)
        mixture = jnp.einsum(
            "hqk,khd->qhd", probability, value_split, preferred_element_type=jnp.float32
        )
        return (
            mixture.reshape(CONT_LEN, width_here).astype(jnp.bfloat16),
            (largest + jnp.log(row_total))[..., 0],
        )

    query_blocks = query_heads.reshape(block_count, CONT_LEN, heads_here, HEAD_DIM)
    mixture, logsum = lax.map(one_block, (query_blocks, row_place_blocks, row_segment_blocks))
    return (mixture.reshape(GROUP_TOK, width_here), logsum)


def attend_backward(query_heads, key_heads, value_heads, grad_heads, logsum, segments):
    block_count = GROUP_TOK // CONT_LEN
    width_here = query_heads.shape[1]
    heads_here = width_here // HEAD_DIM
    key_split = key_heads.reshape(GROUP_TOK, heads_here, HEAD_DIM)
    value_split = value_heads.reshape(GROUP_TOK, heads_here, HEAD_DIM)
    places, prompt_col, row_place_blocks, row_segment_blocks = block_masks(segments)

    def one_block(carry, pieces):
        grad_key_sum, grad_value_sum = carry
        query_block, grad_block, logsum_block, row_places, row_segments = pieces
        scores = jnp.einsum(
            "qhd,khd->hqk", query_block, key_split, preferred_element_type=jnp.float32
        )
        allowed = (places[None, :] <= row_places[:, None]) & (
            prompt_col[None, :] | (segments[None, :] == row_segments[:, None])
        )
        scores = jnp.where(allowed[None], scores, -1e30)
        probability = jnp.exp(scores - logsum_block[..., None])
        upstream = jnp.einsum(
            "qhd,khd->hqk", grad_block, value_split, preferred_element_type=jnp.float32
        )
        centre = jnp.sum(upstream * probability, axis=-1, keepdims=True)
        grad_scores = (probability * (upstream - centre)).astype(jnp.bfloat16)
        grad_query = jnp.einsum(
            "hqk,khd->qhd", grad_scores, key_split, preferred_element_type=jnp.float32
        )
        grad_key_sum = grad_key_sum + jnp.einsum(
            "hqk,qhd->khd", grad_scores, query_block, preferred_element_type=jnp.float32
        )
        grad_value_sum = grad_value_sum + jnp.einsum(
            "hqk,qhd->khd",
            probability.astype(jnp.bfloat16),
            grad_block,
            preferred_element_type=jnp.float32,
        )
        return (
            (grad_key_sum, grad_value_sum),
            grad_query.reshape(CONT_LEN, width_here).astype(jnp.bfloat16),
        )

    query_blocks = query_heads.reshape(block_count, CONT_LEN, heads_here, HEAD_DIM)
    grad_blocks = grad_heads.reshape(block_count, CONT_LEN, heads_here, HEAD_DIM)
    zeros_start = jnp.zeros((GROUP_TOK, heads_here, HEAD_DIM), jnp.float32)
    (grad_key_sum, grad_value_sum), grad_queries = lax.scan(
        one_block,
        (zeros_start, zeros_start),
        (query_blocks, grad_blocks, logsum, row_place_blocks, row_segment_blocks),
    )
    return (
        grad_queries.reshape(GROUP_TOK, width_here),
        grad_key_sum.reshape(GROUP_TOK, width_here).astype(jnp.bfloat16),
        grad_value_sum.reshape(GROUP_TOK, width_here).astype(jnp.bfloat16),
    )


def body(
    inputs,
    cotangent,
    lengths,
    adapter_ids,
    query_weight,
    key_weight,
    value_weight,
    out_weight,
    up_weight,
    down_weight,
    attn_gain,
    mlp_gain,
    query_scale,
    adapter_in,
    adapter_out,
):
    row_count = inputs.shape[1]
    offset = lax.axis_index("heads") * row_count
    segments = segment_of(lengths[0])
    chosen = picker(lax.dynamic_slice_in_dim(segments, offset, row_count), adapter_ids[0])
    flat_down = jnp.transpose(adapter_in, (0, 2, 1, 3)).reshape(4, D, ADAPTERS * RANK)
    flat_up = adapter_out.reshape(4, ADAPTERS * RANK, D)
    gain_attn = attn_gain.astype(jnp.float32)
    gain_mlp = mlp_gain.astype(jnp.float32)
    scale_row = jnp.tile(query_scale, HEADS) * HEAD_DIM ** (-0.5)
    w_query, w_key, w_value, w_out, w_up, w_down = (
        lax.all_gather(query_weight, "fsdp", axis=0, tiled=True),
        lax.all_gather(key_weight, "fsdp", axis=0, tiled=True),
        lax.all_gather(value_weight, "fsdp", axis=0, tiled=True),
        lax.all_gather(out_weight, "fsdp", axis=0, tiled=True),
        lax.all_gather(up_weight, "fsdp", axis=0, tiled=True),
        lax.all_gather(down_weight, "fsdp", axis=0, tiled=True),
    )
    rows_in = inputs[0].astype(jnp.float32)
    normed, scaling_attn = normalize(rows_in, gain_attn)
    normed_low = normed.astype(jnp.bfloat16)
    inner_query, extra_query = adapter_forward(normed_low, flat_down[0], flat_up[0], chosen)
    inner_value, extra_value = adapter_forward(normed_low, flat_down[1], flat_up[1], chosen)
    query_send = ((product(normed_low, w_query) + extra_query) * scale_row).astype(jnp.bfloat16)
    key_send = product(normed_low, w_key).astype(jnp.bfloat16)
    value_send = (product(normed_low, w_value) + extra_value).astype(jnp.bfloat16)
    query_heads, key_heads, value_heads = (
        lax.all_to_all(query_send, "heads", split_axis=1, concat_axis=0, tiled=True),
        lax.all_to_all(key_send, "heads", split_axis=1, concat_axis=0, tiled=True),
        lax.all_to_all(value_send, "heads", split_axis=1, concat_axis=0, tiled=True),
    )
    mixture, logsum = attend_forward(query_heads, key_heads, value_heads, segments)
    mixed_rows = lax.all_to_all(mixture, "heads", split_axis=0, concat_axis=1, tiled=True)
    middle = rows_in + product(mixed_rows, w_out)
    normed_mlp, scaling_mlp = normalize(middle, gain_mlp)
    normed_mlp_low = normed_mlp.astype(jnp.bfloat16)
    inner_up, extra_up = adapter_forward(normed_mlp_low, flat_down[2], flat_up[2], chosen)
    before = product(normed_mlp_low, w_up) + extra_up
    sigmoid_gate = jax.nn.sigmoid(before)
    hidden_low = (before * sigmoid_gate).astype(jnp.bfloat16)
    inner_down, extra_down = adapter_forward(hidden_low, flat_down[3], flat_up[3], chosen)
    outputs = (middle + (product(hidden_low, w_down) + extra_down)).astype(jnp.bfloat16)
    w_query, w_key, w_value, w_out, w_up, w_down = (
        lax.all_gather(query_weight, "fsdp", axis=0, tiled=True),
        lax.all_gather(key_weight, "fsdp", axis=0, tiled=True),
        lax.all_gather(value_weight, "fsdp", axis=0, tiled=True),
        lax.all_gather(out_weight, "fsdp", axis=0, tiled=True),
        lax.all_gather(up_weight, "fsdp", axis=0, tiled=True),
        lax.all_gather(down_weight, "fsdp", axis=0, tiled=True),
    )
    upstream = cotangent[0].astype(jnp.float32)
    grad_after = cotangent[0]
    down_first, down_second, back_down = adapter_backward(
        hidden_low, inner_down, grad_after, flat_down[3], flat_up[3], chosen
    )
    grad_hidden = contract_cols(grad_after, w_down) + back_down
    grad_before = (grad_hidden * sigmoid_gate * (1.0 + before * (1.0 - sigmoid_gate))).astype(
        jnp.bfloat16
    )
    up_first, up_second, back_up = adapter_backward(
        normed_mlp_low, inner_up, grad_before, flat_down[2], flat_up[2], chosen
    )
    grad_normed_mlp = contract_cols(grad_before, w_up) + back_up
    grad_middle = upstream + normalize_back(middle, scaling_mlp, gain_mlp, grad_normed_mlp)
    grad_branch = grad_middle.astype(jnp.bfloat16)
    grad_mixed = contract_cols(grad_branch, w_out).astype(jnp.bfloat16)
    grad_heads = lax.all_to_all(grad_mixed, "heads", split_axis=1, concat_axis=0, tiled=True)
    grad_query_heads, grad_key_heads, grad_value_heads = attend_backward(
        query_heads, key_heads, value_heads, grad_heads, logsum, segments
    )
    grad_query_rows, grad_key_rows, grad_value_rows = (
        lax.all_to_all(grad_query_heads, "heads", split_axis=0, concat_axis=1, tiled=True),
        lax.all_to_all(grad_key_heads, "heads", split_axis=0, concat_axis=1, tiled=True),
        lax.all_to_all(grad_value_heads, "heads", split_axis=0, concat_axis=1, tiled=True),
    )
    grad_query_pre = (grad_query_rows.astype(jnp.float32) * scale_row).astype(jnp.bfloat16)
    query_first, query_second, back_query = adapter_backward(
        normed_low, inner_query, grad_query_pre, flat_down[0], flat_up[0], chosen
    )
    value_first, value_second, back_value = adapter_backward(
        normed_low, inner_value, grad_value_rows, flat_down[1], flat_up[1], chosen
    )
    grad_normed = (
        contract_cols(grad_query_pre, w_query)
        + contract_cols(grad_key_rows, w_key)
        + contract_cols(grad_value_rows, w_value)
        + back_query
        + back_value
    )
    grad_inputs = grad_middle + normalize_back(rows_in, scaling_attn, gain_attn, grad_normed)
    first_terms = jnp.stack([query_first, value_first, up_first, down_first])
    second_terms = jnp.stack([query_second, value_second, up_second, down_second])
    first_total, second_total = lax.psum((first_terms, second_terms), ("heads", "fsdp"))
    grad_first = jnp.transpose(first_total.reshape(4, D, ADAPTERS, RANK), (0, 2, 1, 3))
    grad_second = second_total.reshape(4, ADAPTERS, RANK, D)
    return (outputs[None], grad_inputs[None], grad_first, grad_second)


def solution(mesh):
    placed = (
        P("fsdp", "heads", None),
        P("fsdp", "heads", None),
        P("fsdp", None),
        P("fsdp", None),
        P("fsdp", None),
        P("fsdp", None),
        P("fsdp", None),
        P("fsdp", None),
        P("fsdp", None),
        P("fsdp", None),
        P(),
        P(),
        P(),
        P(),
        P(),
    )
    return jax.shard_map(
        body,
        mesh=mesh,
        in_specs=placed,
        out_specs=(P("fsdp", "heads", None), P("fsdp", "heads", None), P(), P()),
        check_vma=False,
    )
```

profile of v0, /device:TPU:0, one launch (start us, length us, event | category | flops | bytes accessed | tf_op | source)
XLA Modules:
  0.0 1301.6 jit_solution(6721409575038360464)
XLA Ops:
  15.9 35.8 %all-gather.9.cloned.1.call-done = bf16[1280,1280]{1,0:T(8,128)(2,1)} async-done(((bf16[160,1280]{1,0:T(8,128)(2,1)}), bf16[1280,1280]{1,0:T(8,128)(2,1)}) %all-gather.9.cloned.1.call-update) | async-done | bytes 3276816 | tf_op jit(solution)/shard_map/all_gather | solution.py:203
  68.4 23.2 %all-gather.11.cloned.1.call-done = bf16[1280,1280]{1,0:T(8,128)(2,1)} async-done(((bf16[160,1280]{1,0:T(8,128)(2,1)}), bf16[1280,1280]{1,0:T(8,128)(2,1)}) %all-gather.11.cloned.1.call-update) | async-done | bytes 3276816 | tf_op jit(solution)/shard_map/all_gather | solution.py:204
  107.6 23.8 %all-gather.7.cloned.1.call-done = bf16[1280,1280]{1,0:T(8,128)(2,1)} async-done(((bf16[160,1280]{1,0:T(8,128)(2,1)}), bf16[1280,1280]{1,0:T(8,128)(2,1)}) %all-gather.7.cloned.1.call-update) | async-done | bytes 3276816 | tf_op jit(solution)/shard_map/all_gather | solution.py:202
  182.5 230.1 %while.28 = (s32[]{:T(128)}, bf16[6,512,320]{1,2,0:T(8,128)(2,1)}, f32[6,4,512]{2,1,0:T(4,128)}, s32[6,512]{1,0:T(8,128)S(1)}, pred[3072]{0:T(1024)(128)(4,1)S(1...) while((s32[]{:T(128)}, bf16[6,512,320]{1,2,0:T(8,128)(2,1)}, ...), condition=%wide.region_7.8_spmd.clone, body=%wide.region_4.7_spmd.clone.sunk | while | flops 2076342272 | bytes 94989472 | solution.py:115
  488.9 23.0 %all-to-all-done.4 = bf16[768,4,320]{0,2,1:T(8,128)(2,1)} async-done(((bf16[768,4,320]{0,2,1:T(8,128)(2,1)}), bf16[768,4,320]{0,2,1:T(8,128)(2,1)}, u32[]{:S(2)}, u32[]{:S(2)}) %all-to-all-start.4) | async-done | bytes 1966112 | tf_op jit(solution)/shard_map/all_to_all | solution.py:257
  526.7 526.7 %while.29 = (s32[]{:T(128)}, f32[3072,4,80]{0,2,1:T(8,128)}, f32[3072,4,80]{0,2,1:T(8,128)}, bf16[6,512,320]{1,2,0:T(8,128)(2,1)}, bf16[6,512,4,80]{1,3,2,0:T(8,...) while((s32[]{:T(128)}, f32[3072,4,80]{0,2,1:T(8,128)}, ...), condition=%wide.region_12.13_spmd.clone, body=%wide.region_10.12_spmd.clone.sunk | while | flops 5119047680 | bytes 219360688 | solution.py:163
  555.0 17.6 %multiply_reduce_fusion.4 = (f32[4,512]{1,0:T(4,128)S(1)}, f32[4,512,3072]{2,1,0:T(8,128)}) fusion(f32[4,512,3072]{2,1,0:T(8,128)} %fusion.204, f32[4,512]{1,0:T(4,128)S(1)} %dynamic-slice_bitcast_fusion.2, pred[512,3072]{1,0:T(8,128)(4,1)S(1)} %fusion.205, bf16[3072,4,80]{0,2,1:T(8,128)(2,1)} %get-tuple-element.610, ...), kind=kOutput, calls=%fused_computation.20.clone.1 | convolution fusion | flops 1031796736 | bytes 54214660 | tf_op jit(solution)/shard_map/while/body/eval_jaxpr/qhd,khd->hqk/dot_general | solution.py:138
  572.6 21.8 %multiply_convert_fusion.8 = bf16[4,512,3072]{2,1,0:T(8,128)(2,1)} fusion(f32[4,512,3072]{2,1,0:T(8,128)} %get-tuple-element.533, f32[4,512,3072]{2,1,0:T(8,128)} %fusion.204, f32[4,512]{1,0:T(4,128)S(1)} %get-tuple-element.534, f32[4,512]{1,0:T(4,128)S(1)} %dynamic-slice_bitcast_fusion.2, pred[512,3072]{1,0:T(8,128)(4,1)S(1)} %fusion.205), kind=kLoop, calls=%fused_computation.19.clone.1 | loop fusion | flops 31457280 | bytes 64503808 | tf_op jit(solution)/shard_map/while/body/eval_jaxpr/convert_element_type | solution.py:142
  628.1 13.9 %fusion.207 = f32[3072,4,80]{0,2,1:T(8,128)} fusion(f32[4,512,3072]{2,1,0:T(8,128)} %fusion.204, f32[4,512]{1,0:T(4,128)S(1)} %dynamic-slice_bitcast_fusion.2, pred[512,3072]{1,0:T(8,128)(4,1)S(1)} %fusion.205, f32[3072,4,80]{0,2,1:T(8,128)} %get-tuple-element.585, pred[]{:T(512)S(6)} %compare.7, bf16[6,512,4,80]{1,3,2,0:T(8,128)(2,1)} %get-tuple-element.609, ...), kind=kOutput, calls=%fused_computation.32.clone.1 | convolution fusion | flops 1027473408 | bytes 34938884 | tf_op jit(solution)/shard_map/while/body/eval_jaxpr/hqk,qhd->khd/dot_general | solution.py:149
  642.0 17.6 %multiply_reduce_fusion.4 = (f32[4,512]{1,0:T(4,128)S(1)}, f32[4,512,3072]{2,1,0:T(8,128)}) fusion(f32[4,512,3072]{2,1,0:T(8,128)} %fusion.204, f32[4,512]{1,0:T(4,128)S(1)} %dynamic-slice_bitcast_fusion.2, pred[512,3072]{1,0:T(8,128)(4,1)S(1)} %fusion.205, bf16[3072,4,80]{0,2,1:T(8,128)(2,1)} %get-tuple-element.610, ...), kind=kOutput, calls=%fused_computation.20.clone.1 | convolution fusion | flops 1031796736 | bytes 54214660 | tf_op jit(solution)/shard_map/while/body/eval_jaxpr/qhd,khd->hqk/dot_general | solution.py:138
  659.6 21.8 %multiply_convert_fusion.8 = bf16[4,512,3072]{2,1,0:T(8,128)(2,1)} fusion(f32[4,512,3072]{2,1,0:T(8,128)} %get-tuple-element.533, f32[4,512,3072]{2,1,0:T(8,128)} %fusion.204, f32[4,512]{1,0:T(4,128)S(1)} %get-tuple-element.534, f32[4,512]{1,0:T(4,128)S(1)} %dynamic-slice_bitcast_fusion.2, pred[512,3072]{1,0:T(8,128)(4,1)S(1)} %fusion.205), kind=kLoop, calls=%fused_computation.19.clone.1 | loop fusion | flops 31457280 | bytes 64503808 | tf_op jit(solution)/shard_map/while/body/eval_jaxpr/convert_element_type | solution.py:142
  716.2 13.9 %fusion.207 = f32[3072,4,80]{0,2,1:T(8,128)} fusion(f32[4,512,3072]{2,1,0:T(8,128)} %fusion.204, f32[4,512]{1,0:T(4,128)S(1)} %dynamic-slice_bitcast_fusion.2, pred[512,3072]{1,0:T(8,128)(4,1)S(1)} %fusion.205, f32[3072,4,80]{0,2,1:T(8,128)} %get-tuple-element.585, pred[]{:T(512)S(6)} %compare.7, bf16[6,512,4,80]{1,3,2,0:T(8,128)(2,1)} %get-tuple-element.609, ...), kind=kOutput, calls=%fused_computation.32.clone.1 | convolution fusion | flops 1027473408 | bytes 34938884 | tf_op jit(solution)/shard_map/while/body/eval_jaxpr/hqk,qhd->khd/dot_general | solution.py:149
  730.0 17.6 %multiply_reduce_fusion.4 = (f32[4,512]{1,0:T(4,128)S(1)}, f32[4,512,3072]{2,1,0:T(8,128)}) fusion(f32[4,512,3072]{2,1,0:T(8,128)} %fusion.204, f32[4,512]{1,0:T(4,128)S(1)} %dynamic-slice_bitcast_fusion.2, pred[512,3072]{1,0:T(8,128)(4,1)S(1)} %fusion.205, bf16[3072,4,80]{0,2,1:T(8,128)(2,1)} %get-tuple-element.610, ...), kind=kOutput, calls=%fused_computation.20.clone.1 | convolution fusion | flops 1031796736 | bytes 54214660 | tf_op jit(solution)/shard_map/while/body/eval_jaxpr/qhd,khd->hqk/dot_general | solution.py:138
  747.6 21.8 %multiply_convert_fusion.8 = bf16[4,512,3072]{2,1,0:T(8,128)(2,1)} fusion(f32[4,512,3072]{2,1,0:T(8,128)} %get-tuple-element.533, f32[4,512,3072]{2,1,0:T(8,128)} %fusion.204, f32[4,512]{1,0:T(4,128)S(1)} %get-tuple-element.534, f32[4,512]{1,0:T(4,128)S(1)} %dynamic-slice_bitcast_fusion.2, pred[512,3072]{1,0:T(8,128)(4,1)S(1)} %fusion.205), kind=kLoop, calls=%fused_computation.19.clone.1 | loop fusion | flops 31457280 | bytes 64503808 | tf_op jit(solution)/shard_map/while/body/eval_jaxpr/convert_element_type | solution.py:142
  804.2 13.9 %fusion.207 = f32[3072,4,80]{0,2,1:T(8,128)} fusion(f32[4,512,3072]{2,1,0:T(8,128)} %fusion.204, f32[4,512]{1,0:T(4,128)S(1)} %dynamic-slice_bitcast_fusion.2, pred[512,3072]{1,0:T(8,128)(4,1)S(1)} %fusion.205, f32[3072,4,80]{0,2,1:T(8,128)} %get-tuple-element.585, pred[]{:T(512)S(6)} %compare.7, bf16[6,512,4,80]{1,3,2,0:T(8,128)(2,1)} %get-tuple-element.609, ...), kind=kOutput, calls=%fused_computation.32.clone.1 | convolution fusion | flops 1027473408 | bytes 34938884 | tf_op jit(solution)/shard_map/while/body/eval_jaxpr/hqk,qhd->khd/dot_general | solution.py:149
  818.1 17.6 %multiply_reduce_fusion.4 = (f32[4,512]{1,0:T(4,128)S(1)}, f32[4,512,3072]{2,1,0:T(8,128)}) fusion(f32[4,512,3072]{2,1,0:T(8,128)} %fusion.204, f32[4,512]{1,0:T(4,128)S(1)} %dynamic-slice_bitcast_fusion.2, pred[512,3072]{1,0:T(8,128)(4,1)S(1)} %fusion.205, bf16[3072,4,80]{0,2,1:T(8,128)(2,1)} %get-tuple-element.610, ...), kind=kOutput, calls=%fused_computation.20.clone.1 | convolution fusion | flops 1031796736 | bytes 54214660 | tf_op jit(solution)/shard_map/while/body/eval_jaxpr/qhd,khd->hqk/dot_general | solution.py:138
  835.7 21.8 %multiply_convert_fusion.8 = bf16[4,512,3072]{2,1,0:T(8,128)(2,1)} fusion(f32[4,512,3072]{2,1,0:T(8,128)} %get-tuple-element.533, f32[4,512,3072]{2,1,0:T(8,128)} %fusion.204, f32[4,512]{1,0:T(4,128)S(1)} %get-tuple-element.534, f32[4,512]{1,0:T(4,128)S(1)} %dynamic-slice_bitcast_fusion.2, pred[512,3072]{1,0:T(8,128)(4,1)S(1)} %fusion.205), kind=kLoop, calls=%fused_computation.19.clone.1 | loop fusion | flops 31457280 | bytes 64503808 | tf_op jit(solution)/shard_map/while/body/eval_jaxpr/convert_element_type | solution.py:142
  892.3 13.9 %fusion.207 = f32[3072,4,80]{0,2,1:T(8,128)} fusion(f32[4,512,3072]{2,1,0:T(8,128)} %fusion.204, f32[4,512]{1,0:T(4,128)S(1)} %dynamic-slice_bitcast_fusion.2, pred[512,3072]{1,0:T(8,128)(4,1)S(1)} %fusion.205, f32[3072,4,80]{0,2,1:T(8,128)} %get-tuple-element.585, pred[]{:T(512)S(6)} %compare.7, bf16[6,512,4,80]{1,3,2,0:T(8,128)(2,1)} %get-tuple-element.609, ...), kind=kOutput, calls=%fused_computation.32.clone.1 | convolution fusion | flops 1027473408 | bytes 34938884 | tf_op jit(solution)/shard_map/while/body/eval_jaxpr/hqk,qhd->khd/dot_general | solution.py:149
  906.2 17.6 %multiply_reduce_fusion.4 = (f32[4,512]{1,0:T(4,128)S(1)}, f32[4,512,3072]{2,1,0:T(8,128)}) fusion(f32[4,512,3072]{2,1,0:T(8,128)} %fusion.204, f32[4,512]{1,0:T(4,128)S(1)} %dynamic-slice_bitcast_fusion.2, pred[512,3072]{1,0:T(8,128)(4,1)S(1)} %fusion.205, bf16[3072,4,80]{0,2,1:T(8,128)(2,1)} %get-tuple-element.610, ...), kind=kOutput, calls=%fused_computation.20.clone.1 | convolution fusion | flops 1031796736 | bytes 54214660 | tf_op jit(solution)/shard_map/while/body/eval_jaxpr/qhd,khd->hqk/dot_general | solution.py:138
  923.8 21.8 %multiply_convert_fusion.8 = bf16[4,512,3072]{2,1,0:T(8,128)(2,1)} fusion(f32[4,512,3072]{2,1,0:T(8,128)} %get-tuple-element.533, f32[4,512,3072]{2,1,0:T(8,128)} %fusion.204, f32[4,512]{1,0:T(4,128)S(1)} %get-tuple-element.534, f32[4,512]{1,0:T(4,128)S(1)} %dynamic-slice_bitcast_fusion.2, pred[512,3072]{1,0:T(8,128)(4,1)S(1)} %fusion.205), kind=kLoop, calls=%fused_computation.19.clone.1 | loop fusion | flops 31457280 | bytes 64503808 | tf_op jit(solution)/shard_map/while/body/eval_jaxpr/convert_element_type | solution.py:142
  980.4 13.9 %fusion.207 = f32[3072,4,80]{0,2,1:T(8,128)} fusion(f32[4,512,3072]{2,1,0:T(8,128)} %fusion.204, f32[4,512]{1,0:T(4,128)S(1)} %dynamic-slice_bitcast_fusion.2, pred[512,3072]{1,0:T(8,128)(4,1)S(1)} %fusion.205, f32[3072,4,80]{0,2,1:T(8,128)} %get-tuple-element.585, pred[]{:T(512)S(6)} %compare.7, bf16[6,512,4,80]{1,3,2,0:T(8,128)(2,1)} %get-tuple-element.609, ...), kind=kOutput, calls=%fused_computation.32.clone.1 | convolution fusion | flops 1027473408 | bytes 34938884 | tf_op jit(solution)/shard_map/while/body/eval_jaxpr/hqk,qhd->khd/dot_general | solution.py:149
  994.2 17.6 %multiply_reduce_fusion.4 = (f32[4,512]{1,0:T(4,128)S(1)}, f32[4,512,3072]{2,1,0:T(8,128)}) fusion(f32[4,512,3072]{2,1,0:T(8,128)} %fusion.204, f32[4,512]{1,0:T(4,128)S(1)} %dynamic-slice_bitcast_fusion.2, pred[512,3072]{1,0:T(8,128)(4,1)S(1)} %fusion.205, bf16[3072,4,80]{0,2,1:T(8,128)(2,1)} %get-tuple-element.610, ...), kind=kOutput, calls=%fused_computation.20.clone.1 | convolution fusion | flops 1031796736 | bytes 54214660 | tf_op jit(solution)/shard_map/while/body/eval_jaxpr/qhd,khd->hqk/dot_general | solution.py:138
  1011.8 21.8 %multiply_convert_fusion.8 = bf16[4,512,3072]{2,1,0:T(8,128)(2,1)} fusion(f32[4,512,3072]{2,1,0:T(8,128)} %get-tuple-element.533, f32[4,512,3072]{2,1,0:T(8,128)} %fusion.204, f32[4,512]{1,0:T(4,128)S(1)} %get-tuple-element.534, f32[4,512]{1,0:T(4,128)S(1)} %dynamic-slice_bitcast_fusion.2, pred[512,3072]{1,0:T(8,128)(4,1)S(1)} %fusion.205), kind=kLoop, calls=%fused_computation.19.clone.1 | loop fusion | flops 31457280 | bytes 64503808 | tf_op jit(solution)/shard_map/while/body/eval_jaxpr/convert_element_type | solution.py:142
  1167.7 121.7 %all-reduce.3.cloned.1.call-done = (f32[4,8,1280,16]{2,3,1,0:T(8,128)}, f32[4,8,16,1280]{3,2,1,0:T(8,128)}) async-done(((f32[4,8,1280,16]{2,3,1,0:T(8,128)}, f32[4,8,16,1280]{3,2,1,0:T(8,128)}), (f32[4,8,1280,16]{2,3,1,0:T(8,128)}, f32[4,8,16,1280]{3,2,1,0:T(8,128)})) %all-reduce.3.cloned.1.call-update) | async-done | bytes 5242896 | tf_op jit(solution)/shard_map/psum | solution.py:283
  (483 shorter events, 751.3 us)
Async XLA Ops:
  7.2 44.5 %all-gather.9.cloned.1.call-start = ((), (), s32[]{:S(2)}) async-start(), calls=%async_computation.9 | async-start | bytes 3686400 | tf_op jit(solution)/shard_map/all_gather | solution.py:203
  7.9 83.6 %all-gather.11.cloned.1.call-start = ((), (), s32[]{:S(2)}) async-start(), calls=%async_computation.10 | async-start | bytes 3686400 | tf_op jit(solution)/shard_map/all_gather | solution.py:204
  8.7 122.8 %all-gather.7.cloned.1.call-start = ((), (), s32[]{:S(2)}) async-start(), calls=%async_computation.8 | async-start | bytes 3686400 | tf_op jit(solution)/shard_map/all_gather | solution.py:202
  9.4 418.7 %all-gather.17.cloned.1.call-start = ((), (), s32[]{:S(2)}) async-start(), calls=%async_computation.13 | async-start | bytes 3686400 | tf_op jit(solution)/shard_map/all_gather | solution.py:207
  10.0 425.4 %all-gather.13.cloned.1.call-start = ((), (), s32[]{:S(2)}) async-start(), calls=%async_computation.11 | async-start | bytes 3686400 | tf_op jit(solution)/shard_map/all_gather | solution.py:205
  12.5 118.9 %copy-start.68 = (f32[768]{0:T(1024)}, f32[768]{0:T(1024)S(1)}, u32[]{:S(2)}) copy-start(f32[768]{0:T(1024)S(1)} %get-tuple-element.366) | copy-start | bytes 9220
  12.5 118.9 %copy-start.65 = (f32[1280]{0:T(1024)}, f32[1280]{0:T(1024)S(1)}, u32[]{:S(2)}) copy-start(f32[1280]{0:T(1024)S(1)} %convert_element_type.166) | copy-start | bytes 15364
  12.8 94.0 %copy-start.76 = (s32[768]{0:T(1024)}, s32[768]{0:T(1024)S(1)}, u32[]{:S(2)}) copy-start(s32[768]{0:T(1024)S(1)} %select_reduce_fusion.1) | copy-start | bytes 9220
  12.8 94.0 %copy-start.85 = (s32[128]{0:T(128)}, s32[128]{0:T(128)S(1)}, u32[]{:S(2)}) copy-start(s32[128]{0:T(128)S(1)} %and_select_fusion) | copy-start | bytes 1540
  15.1 42.6 %copy-start.30 = (bf16[1,1280,8,16]{1,3,2,0:T(8,128)(2,1)}, bf16[1,1280,8,16]{1,3,2,0:T(8,128)(2,1)S(1)}, u32[]{:S(2)}) copy-start(bf16[1,1280,8,16]{1,3,2,0:T(8,128)(2,1)S(1)} %get-tuple-element.361) | copy-start | bytes 983044
  15.1 91.8 %copy-start.39 = (bf16[1,1280,8,16]{1,3,2,0:T(8,128)(2,1)}, bf16[1,1280,8,16]{1,3,2,0:T(8,128)(2,1)S(1)}, u32[]{:S(2)}) copy-start(bf16[1,1280,8,16]{1,3,2,0:T(8,128)(2,1)S(1)} %get-tuple-element.362) | copy-start | bytes 983044
  15.8 80.4 %copy-start.43 = (bf16[768,128]{1,0:T(8,128)(2,1)}, bf16[768,128]{1,0:T(8,128)(2,1)S(1)}, u32[]{:S(2)}) copy-start(bf16[768,128]{1,0:T(8,128)(2,1)S(1)} %fusion.79) | copy-start | bytes 589828
  61.7 40.6 %all-to-all-start.1 = ((bf16[768,4,320]{0,2,1:T(8,128)(2,1)}), bf16[768,4,320]{0,2,1:T(8,128)(2,1)}, u32[]{:S(2)}, u32[]{:S(2)}) async-start(bf16[768,4,320]{0,2,1:T(8,128)(2,1)} %bitcast.288), calls=%async_computation.1 | async-start | bytes 3932160 | tf_op jit(solution)/shard_map/all_to_all | solution.py:219
  68.4 67.8 %copy-start.32 = (bf16[1,8,16,1280]{3,2,1,0:T(8,128)(2,1)}, bf16[1,8,16,1280]{3,2,1,0:T(8,128)(2,1)S(1)}, u32[]{:S(2)}) copy-start(bf16[1,8,16,1280]{3,2,1,0:T(8,128)(2,1)S(1)} %get-tuple-element.357) | copy-start | bytes 983044
  102.3 36.8 %all-to-all-start.2 = ((bf16[768,4,320]{0,2,1:T(8,128)(2,1)}), bf16[768,4,320]{0,2,1:T(8,128)(2,1)}, u32[]{:S(2)}, u32[]{:S(2)}) async-start(bf16[768,4,320]{0,2,1:T(8,128)(2,1)} %bitcast.287), calls=%async_computation.2 | async-start | bytes 3932160 | tf_op jit(solution)/shard_map/all_to_all | solution.py:220
  139.1 28.6 %all-to-all-start = ((bf16[768,4,320]{0,2,1:T(8,128)(2,1)}), bf16[768,4,320]{0,2,1:T(8,128)(2,1)}, u32[]{:S(2)}, u32[]{:S(2)}) async-start(bf16[768,4,320]{0,2,1:T(8,128)(2,1)} %bitcast.8), calls=%async_computation | async-start | bytes 3932160 | tf_op jit(solution)/shard_map/all_to_all | solution.py:218
  143.6 315.5 %all-gather.15.cloned.1.call-start = ((), (), s32[]{:S(2)}) async-start(), calls=%async_computation.12 | async-start | bytes 3686400 | tf_op jit(solution)/shard_map/all_gather | solution.py:206
  420.9 27.7 %all-to-all-start.3 = ((bf16[4,768,320]{1,2,0:T(8,128)(2,1)}), bf16[4,768,320]{1,2,0:T(8,128)(2,1)}, u32[]{:S(2)}, u32[]{:S(2)}) async-start(bf16[4,768,320]{1,2,0:T(8,128)(2,1)} %copy.81), calls=%async_computation.3 | async-start | bytes 3932160 | tf_op jit(solution)/shard_map/all_to_all | solution.py:223
  428.1 38.8 %copy-start.53 = (bf16[768,128]{1,0:T(8,128)(2,1)}, bf16[768,128]{1,0:T(8,128)(2,1)S(1)}, u32[]{:S(2)}) copy-start(bf16[768,128]{1,0:T(8,128)(2,1)S(1)} %fusion.85) | copy-start | bytes 589828
  484.4 27.5 %all-to-all-start.4 = ((bf16[768,4,320]{0,2,1:T(8,128)(2,1)}), bf16[768,4,320]{0,2,1:T(8,128)(2,1)}, u32[]{:S(2)}, u32[]{:S(2)}) async-start(bf16[768,4,320]{0,2,1:T(8,128)(2,1)} %bitcast.289), calls=%async_computation.4 | async-start | bytes 3932160 | tf_op jit(solution)/shard_map/all_to_all | solution.py:257
  1061.4 27.6 %all-to-all-start.7 = ((bf16[4,768,320]{1,2,0:T(8,128)(2,1)}), bf16[4,768,320]{1,2,0:T(8,128)(2,1)}, u32[]{:S(2)}, u32[]{:S(2)}) async-start(bf16[4,768,320]{1,2,0:T(8,128)(2,1)} %copy.90), calls=%async_computation.7 | async-start | bytes 3932160 | tf_op jit(solution)/shard_map/all_to_all | solution.py:264
  1089.0 26.7 %all-to-all-start.5 = ((bf16[4,768,320]{1,2,0:T(8,128)(2,1)}), bf16[4,768,320]{1,2,0:T(8,128)(2,1)S(1)}, u32[]{:S(2)}, u32[]{:S(2)}) async-start(bf16[4,768,320]{1,2,0:T(8,128)(2,1)} %copy.87), calls=%async_computation.5 | async-start | bytes 3932160 | tf_op jit(solution)/shard_map/all_to_all | solution.py:262
  1117.0 36.9 %all-to-all-start.6 = ((bf16[4,768,320]{1,2,0:T(8,128)(2,1)}), bf16[4,768,320]{1,2,0:T(8,128)(2,1)}, u32[]{:S(2)}, u32[]{:S(2)}) async-start(bf16[4,768,320]{1,2,0:T(8,128)(2,1)} %copy.89), calls=%async_computation.6 | async-start | bytes 3932160 | tf_op jit(solution)/shard_map/all_to_all | solution.py:263
  1121.5 168.0 %all-reduce.3.cloned.1.call-start = ((), (), s32[]{:S(2)}) async-start(), calls=%async_computation.14 | async-start | bytes 10485760 | tf_op jit(solution)/shard_map/psum | solution.py:283
  (125 other events, 875.1 us)
Sparse Core Ops, SparseCore 0:
  9.6 42.0 all-gather.8
  53.3 38.1 all-gather.10
  93.2 38.1 all-gather.6
  132.9 38.1 all-gather.16
  172.6 38.1 all-gather.12
  212.4 38.1 all-gather.14
  1141.9 147.4 all-reduce.2
where the time goes:
time: 1310 us; the launch traced here: 1300 us
  matrix products  603 us (46%)
  waiting for transfers between devices  260 us (20%)
  other arithmetic  252 us (19%)
  local copies, waits for them, and re-layouts  133 us (10%)
  starting transfers between devices  35.6 us (3%)
  between operations  15.4 us (1%)
    dot_general x12, matrix products, one_block(): jnp.einsum('qhd,khd->hqk', query_block, key_split, preferred_element_type...  137 us
    convert_element_type x6, other arithmetic, one_block(): grad_scores = (probability * (upstream - centre)).astype(jnp.bfloat16)  131 us
    psum x1, waiting for transfers between devices, body(): lax.psum((first_terms, second_terms), ('heads', 'fsdp'))  122 us
    dot_general x6, matrix products, one_block(): jnp.einsum('qhd,khd->hqk', grad_block, value_split, preferred_element_typ...  106 us
    dot_general x6, matrix products, one_block(): jnp.einsum('hqk,qhd->khd', probability.astype(jnp.bfloat16), grad_block,...  82 us
    reduce_sum x6, other arithmetic, one_block(): row_total = jnp.sum(exponent, axis=-1, keepdims=True)  70.7 us
    dot_general x6, matrix products, one_block(): jnp.einsum('hqk,khd->qhd', probability, value_split, preferred_element_ty...  68.5 us
    dot_general x6, matrix products, one_block(): jnp.einsum('hqk,qhd->khd', grad_scores, query_block, preferred_element_ty...  59.4 us
  transfers between devices with their start and end apart: 15, of which 8 were waited for; matrix products, arithmetic and copies ran while one was open for 31% of the time, Pallas kernels for 0%

commit v1 on v0

--- a/solution.py
+++ b/solution.py
@@ -254,7 +254,12 @@
     grad_middle = upstream + normalize_back(middle, scaling_mlp, gain_mlp, grad_normed_mlp)
     grad_branch = grad_middle.astype(jnp.bfloat16)
     grad_mixed = contract_cols(grad_branch, w_out).astype(jnp.bfloat16)
-    grad_heads = lax.all_to_all(grad_mixed, "heads", split_axis=1, concat_axis=0, tiled=True)
+    grad_heads = jnp.concatenate(
+        lax.all_to_all(
+            jnp.stack(jnp.split(grad_mixed, lax.psum(1, "heads"), axis=1), axis=0), "heads", 0, 0
+        ),
+        axis=0,
+    )
     grad_query_heads, grad_key_heads, grad_value_heads = attend_backward(
         query_heads, key_heads, value_heads, grad_heads, logsum, segments
     )

time: 1310 us -> 1310 us (level)
  no operation moved by 1% of the time
where the time goes in v1:
time: 1310 us; the launch traced here: 1300 us
  matrix products  603 us (46%)
  waiting for transfers between devices  261 us (20%)
  other arithmetic  254 us (19%)
  local copies, waits for them, and re-layouts  134 us (10%)
  starting transfers between devices  35.6 us (3%)
  between operations  15.5 us (1%)
    dot_general x12, matrix products, one_block(): jnp.einsum('qhd,khd->hqk', query_block, key_split, preferred_element_type...  138 us
    convert_element_type x6, other arithmetic, one_block(): grad_scores = (probability * (upstream - centre)).astype(jnp.bfloat16)  131 us
    psum x1, waiting for transfers between devices, body(): lax.psum((first_terms, second_terms), ('heads', 'fsdp'))  122 us
    dot_general x6, matrix products, one_block(): jnp.einsum('qhd,khd->hqk', grad_block, value_split, preferred_element_typ...  106 us
    dot_general x6, matrix products, one_block(): jnp.einsum('hqk,qhd->khd', probability.astype(jnp.bfloat16), grad_block,...  81.9 us
    reduce_sum x6, other arithmetic, one_block(): row_total = jnp.sum(exponent, axis=-1, keepdims=True)  70.7 us
    dot_general x6, matrix products, one_block(): jnp.einsum('hqk,khd->qhd', probability, value_split, preferred_element_ty...  68.5 us
    dot_general x6, matrix products, one_block(): jnp.einsum('hqk,qhd->khd', grad_scores, query_block, preferred_element_ty...  59.4 us
  transfers between devices with their start and end apart: 15, of which 8 were waited for; matrix products, arithmetic and copies ran while one was open for 31% of the time, Pallas kernels for 0%

profile of v1, /device:TPU:0, one launch (start us, length us, event | category | flops | bytes accessed | tf_op | source)
XLA Modules:
  0.0 1303.6 jit_solution(4335301740198018552)
XLA Ops:
  15.9 35.8 %all-gather.9.cloned.1.call-done = bf16[1280,1280]{1,0:T(8,128)(2,1)} async-done(((bf16[160,1280]{1,0:T(8,128)(2,1)}), bf16[1280,1280]{1,0:T(8,128)(2,1)}) %all-gather.9.cloned.1.call-update) | async-done | bytes 3276816 | tf_op jit(solution)/shard_map/all_gather | solution.py:203
  68.4 23.2 %all-gather.11.cloned.1.call-done = bf16[1280,1280]{1,0:T(8,128)(2,1)} async-done(((bf16[160,1280]{1,0:T(8,128)(2,1)}), bf16[1280,1280]{1,0:T(8,128)(2,1)}) %all-gather.11.cloned.1.call-update) | async-done | bytes 3276816 | tf_op jit(solution)/shard_map/all_gather | solution.py:204
  107.6 23.8 %all-gather.7.cloned.1.call-done = bf16[1280,1280]{1,0:T(8,128)(2,1)} async-done(((bf16[160,1280]{1,0:T(8,128)(2,1)}), bf16[1280,1280]{1,0:T(8,128)(2,1)}) %all-gather.7.cloned.1.call-update) | async-done | bytes 3276816 | tf_op jit(solution)/shard_map/all_gather | solution.py:202
  182.6 230.2 %while.28 = (s32[]{:T(128)}, bf16[6,512,320]{1,2,0:T(8,128)(2,1)}, f32[6,4,512]{2,1,0:T(4,128)}, s32[6,512]{1,0:T(8,128)S(1)}, pred[3072]{0:T(1024)(128)(4,1)S(1...) while((s32[]{:T(128)}, bf16[6,512,320]{1,2,0:T(8,128)(2,1)}, ...), condition=%wide.region_7.8_spmd.clone, body=%wide.region_4.7_spmd.clone.sunk | while | flops 2076342272 | bytes 94989472 | solution.py:115
  490.8 23.0 %all-to-all-done.4 = bf16[4,768,320]{1,2,0:T(8,128)(2,1)} async-done(((bf16[4,768,320]{1,2,0:T(8,128)(2,1)}), bf16[4,768,320]{1,2,0:T(8,128)(2,1)}, u32[]{:S(2)}, u32[]{:S(2)}) %all-to-all-start.4) | async-done | bytes 1966112 | tf_op jit(solution)/shard_map/all_to_all | solution.py:258
  528.7 526.7 %while.29 = (s32[]{:T(128)}, f32[3072,4,80]{0,2,1:T(8,128)}, f32[3072,4,80]{0,2,1:T(8,128)}, bf16[6,512,320]{1,2,0:T(8,128)(2,1)}, bf16[6,512,4,80]{1,3,2,0:T(8,...) while((s32[]{:T(128)}, f32[3072,4,80]{0,2,1:T(8,128)}, ...), condition=%wide.region_12.13_spmd.clone, body=%wide.region_10.12_spmd.clone.sunk | while | flops 5119047680 | bytes 219360688 | solution.py:163
  557.1 17.6 %multiply_reduce_fusion.4 = (f32[4,512]{1,0:T(4,128)S(1)}, f32[4,512,3072]{2,1,0:T(8,128)}) fusion(f32[4,512,3072]{2,1,0:T(8,128)} %fusion.204, f32[4,512]{1,0:T(4,128)S(1)} %dynamic-slice_bitcast_fusion.2, pred[512,3072]{1,0:T(8,128)(4,1)S(1)} %fusion.205, bf16[3072,4,80]{0,2,1:T(8,128)(2,1)} %get-tuple-element.627, ...), kind=kOutput, calls=%fused_computation.20.clone.1 | convolution fusion | flops 1031796736 | bytes 54214660 | tf_op jit(solution)/shard_map/while/body/eval_jaxpr/qhd,khd->hqk/dot_general | solution.py:138
  574.6 21.8 %multiply_convert_fusion.8 = bf16[4,512,3072]{2,1,0:T(8,128)(2,1)} fusion(f32[4,512,3072]{2,1,0:T(8,128)} %get-tuple-element.550, f32[4,512,3072]{2,1,0:T(8,128)} %fusion.204, f32[4,512]{1,0:T(4,128)S(1)} %get-tuple-element.551, f32[4,512]{1,0:T(4,128)S(1)} %dynamic-slice_bitcast_fusion.2, pred[512,3072]{1,0:T(8,128)(4,1)S(1)} %fusion.205), kind=kLoop, calls=%fused_computation.19.clone.1 | loop fusion | flops 31457280 | bytes 64503808 | tf_op jit(solution)/shard_map/while/body/eval_jaxpr/convert_element_type | solution.py:142
  630.1 13.8 %fusion.207 = f32[3072,4,80]{0,2,1:T(8,128)} fusion(f32[4,512,3072]{2,1,0:T(8,128)} %fusion.204, f32[4,512]{1,0:T(4,128)S(1)} %dynamic-slice_bitcast_fusion.2, pred[512,3072]{1,0:T(8,128)(4,1)S(1)} %fusion.205, f32[3072,4,80]{0,2,1:T(8,128)} %get-tuple-element.602, pred[]{:T(512)S(6)} %compare.7, bf16[6,512,4,80]{1,3,2,0:T(8,128)(2,1)} %get-tuple-element.626, ...), kind=kOutput, calls=%fused_computation.32.clone.1 | convolution fusion | flops 1027473408 | bytes 34938884 | tf_op jit(solution)/shard_map/while/body/eval_jaxpr/hqk,qhd->khd/dot_general | solution.py:149
  644.0 17.6 %multiply_reduce_fusion.4 = (f32[4,512]{1,0:T(4,128)S(1)}, f32[4,512,3072]{2,1,0:T(8,128)}) fusion(f32[4,512,3072]{2,1,0:T(8,128)} %fusion.204, f32[4,512]{1,0:T(4,128)S(1)} %dynamic-slice_bitcast_fusion.2, pred[512,3072]{1,0:T(8,128)(4,1)S(1)} %fusion.205, bf16[3072,4,80]{0,2,1:T(8,128)(2,1)} %get-tuple-element.627, ...), kind=kOutput, calls=%fused_computation.20.clone.1 | convolution fusion | flops 1031796736 | bytes 54214660 | tf_op jit(solution)/shard_map/while/body/eval_jaxpr/qhd,khd->hqk/dot_general | solution.py:138
  661.6 21.8 %multiply_convert_fusion.8 = bf16[4,512,3072]{2,1,0:T(8,128)(2,1)} fusion(f32[4,512,3072]{2,1,0:T(8,128)} %get-tuple-element.550, f32[4,512,3072]{2,1,0:T(8,128)} %fusion.204, f32[4,512]{1,0:T(4,128)S(1)} %get-tuple-element.551, f32[4,512]{1,0:T(4,128)S(1)} %dynamic-slice_bitcast_fusion.2, pred[512,3072]{1,0:T(8,128)(4,1)S(1)} %fusion.205), kind=kLoop, calls=%fused_computation.19.clone.1 | loop fusion | flops 31457280 | bytes 64503808 | tf_op jit(solution)/shard_map/while/body/eval_jaxpr/convert_element_type | solution.py:142
  718.2 13.8 %fusion.207 = f32[3072,4,80]{0,2,1:T(8,128)} fusion(f32[4,512,3072]{2,1,0:T(8,128)} %fusion.204, f32[4,512]{1,0:T(4,128)S(1)} %dynamic-slice_bitcast_fusion.2, pred[512,3072]{1,0:T(8,128)(4,1)S(1)} %fusion.205, f32[3072,4,80]{0,2,1:T(8,128)} %get-tuple-element.602, pred[]{:T(512)S(6)} %compare.7, bf16[6,512,4,80]{1,3,2,0:T(8,128)(2,1)} %get-tuple-element.626, ...), kind=kOutput, calls=%fused_computation.32.clone.1 | convolution fusion | flops 1027473408 | bytes 34938884 | tf_op jit(solution)/shard_map/while/body/eval_jaxpr/hqk,qhd->khd/dot_general | solution.py:149
  732.0 17.6 %multiply_reduce_fusion.4 = (f32[4,512]{1,0:T(4,128)S(1)}, f32[4,512,3072]{2,1,0:T(8,128)}) fusion(f32[4,512,3072]{2,1,0:T(8,128)} %fusion.204, f32[4,512]{1,0:T(4,128)S(1)} %dynamic-slice_bitcast_fusion.2, pred[512,3072]{1,0:T(8,128)(4,1)S(1)} %fusion.205, bf16[3072,4,80]{0,2,1:T(8,128)(2,1)} %get-tuple-element.627, ...), kind=kOutput, calls=%fused_computation.20.clone.1 | convolution fusion | flops 1031796736 | bytes 54214660 | tf_op jit(solution)/shard_map/while/body/eval_jaxpr/qhd,khd->hqk/dot_general | solution.py:138
  749.6 21.8 %multiply_convert_fusion.8 = bf16[4,512,3072]{2,1,0:T(8,128)(2,1)} fusion(f32[4,512,3072]{2,1,0:T(8,128)} %get-tuple-element.550, f32[4,512,3072]{2,1,0:T(8,128)} %fusion.204, f32[4,512]{1,0:T(4,128)S(1)} %get-tuple-element.551, f32[4,512]{1,0:T(4,128)S(1)} %dynamic-slice_bitcast_fusion.2, pred[512,3072]{1,0:T(8,128)(4,1)S(1)} %fusion.205), kind=kLoop, calls=%fused_computation.19.clone.1 | loop fusion | flops 31457280 | bytes 64503808 | tf_op jit(solution)/shard_map/while/body/eval_jaxpr/convert_element_type | solution.py:142
  806.2 13.8 %fusion.207 = f32[3072,4,80]{0,2,1:T(8,128)} fusion(f32[4,512,3072]{2,1,0:T(8,128)} %fusion.204, f32[4,512]{1,0:T(4,128)S(1)} %dynamic-slice_bitcast_fusion.2, pred[512,3072]{1,0:T(8,128)(4,1)S(1)} %fusion.205, f32[3072,4,80]{0,2,1:T(8,128)} %get-tuple-element.602, pred[]{:T(512)S(6)} %compare.7, bf16[6,512,4,80]{1,3,2,0:T(8,128)(2,1)} %get-tuple-element.626, ...), kind=kOutput, calls=%fused_computation.32.clone.1 | convolution fusion | flops 1027473408 | bytes 34938884 | tf_op jit(solution)/shard_map/while/body/eval_jaxpr/hqk,qhd->khd/dot_general | solution.py:149
  820.0 17.6 %multiply_reduce_fusion.4 = (f32[4,512]{1,0:T(4,128)S(1)}, f32[4,512,3072]{2,1,0:T(8,128)}) fusion(f32[4,512,3072]{2,1,0:T(8,128)} %fusion.204, f32[4,512]{1,0:T(4,128)S(1)} %dynamic-slice_bitcast_fusion.2, pred[512,3072]{1,0:T(8,128)(4,1)S(1)} %fusion.205, bf16[3072,4,80]{0,2,1:T(8,128)(2,1)} %get-tuple-element.627, ...), kind=kOutput, calls=%fused_computation.20.clone.1 | convolution fusion | flops 1031796736 | bytes 54214660 | tf_op jit(solution)/shard_map/while/body/eval_jaxpr/qhd,khd->hqk/dot_general | solution.py:138
  837.6 21.8 %multiply_convert_fusion.8 = bf16[4,512,3072]{2,1,0:T(8,128)(2,1)} fusion(f32[4,512,3072]{2,1,0:T(8,128)} %get-tuple-element.550, f32[4,512,3072]{2,1,0:T(8,128)} %fusion.204, f32[4,512]{1,0:T(4,128)S(1)} %get-tuple-element.551, f32[4,512]{1,0:T(4,128)S(1)} %dynamic-slice_bitcast_fusion.2, pred[512,3072]{1,0:T(8,128)(4,1)S(1)} %fusion.205), kind=kLoop, calls=%fused_computation.19.clone.1 | loop fusion | flops 31457280 | bytes 64503808 | tf_op jit(solution)/shard_map/while/body/eval_jaxpr/convert_element_type | solution.py:142
  894.2 13.8 %fusion.207 = f32[3072,4,80]{0,2,1:T(8,128)} fusion(f32[4,512,3072]{2,1,0:T(8,128)} %fusion.204, f32[4,512]{1,0:T(4,128)S(1)} %dynamic-slice_bitcast_fusion.2, pred[512,3072]{1,0:T(8,128)(4,1)S(1)} %fusion.205, f32[3072,4,80]{0,2,1:T(8,128)} %get-tuple-element.602, pred[]{:T(512)S(6)} %compare.7, bf16[6,512,4,80]{1,3,2,0:T(8,128)(2,1)} %get-tuple-element.626, ...), kind=kOutput, calls=%fused_computation.32.clone.1 | convolution fusion | flops 1027473408 | bytes 34938884 | tf_op jit(solution)/shard_map/while/body/eval_jaxpr/hqk,qhd->khd/dot_general | solution.py:149
  908.1 17.6 %multiply_reduce_fusion.4 = (f32[4,512]{1,0:T(4,128)S(1)}, f32[4,512,3072]{2,1,0:T(8,128)}) fusion(f32[4,512,3072]{2,1,0:T(8,128)} %fusion.204, f32[4,512]{1,0:T(4,128)S(1)} %dynamic-slice_bitcast_fusion.2, pred[512,3072]{1,0:T(8,128)(4,1)S(1)} %fusion.205, bf16[3072,4,80]{0,2,1:T(8,128)(2,1)} %get-tuple-element.627, ...), kind=kOutput, calls=%fused_computation.20.clone.1 | convolution fusion | flops 1031796736 | bytes 54214660 | tf_op jit(solution)/shard_map/while/body/eval_jaxpr/qhd,khd->hqk/dot_general | solution.py:138
  925.7 21.8 %multiply_convert_fusion.8 = bf16[4,512,3072]{2,1,0:T(8,128)(2,1)} fusion(f32[4,512,3072]{2,1,0:T(8,128)} %get-tuple-element.550, f32[4,512,3072]{2,1,0:T(8,128)} %fusion.204, f32[4,512]{1,0:T(4,128)S(1)} %get-tuple-element.551, f32[4,512]{1,0:T(4,128)S(1)} %dynamic-slice_bitcast_fusion.2, pred[512,3072]{1,0:T(8,128)(4,1)S(1)} %fusion.205), kind=kLoop, calls=%fused_computation.19.clone.1 | loop fusion | flops 31457280 | bytes 64503808 | tf_op jit(solution)/shard_map/while/body/eval_jaxpr/convert_element_type | solution.py:142
  982.3 13.8 %fusion.207 = f32[3072,4,80]{0,2,1:T(8,128)} fusion(f32[4,512,3072]{2,1,0:T(8,128)} %fusion.204, f32[4,512]{1,0:T(4,128)S(1)} %dynamic-slice_bitcast_fusion.2, pred[512,3072]{1,0:T(8,128)(4,1)S(1)} %fusion.205, f32[3072,4,80]{0,2,1:T(8,128)} %get-tuple-element.602, pred[]{:T(512)S(6)} %compare.7, bf16[6,512,4,80]{1,3,2,0:T(8,128)(2,1)} %get-tuple-element.626, ...), kind=kOutput, calls=%fused_computation.32.clone.1 | convolution fusion | flops 1027473408 | bytes 34938884 | tf_op jit(solution)/shard_map/while/body/eval_jaxpr/hqk,qhd->khd/dot_general | solution.py:149
  996.1 17.6 %multiply_reduce_fusion.4 = (f32[4,512]{1,0:T(4,128)S(1)}, f32[4,512,3072]{2,1,0:T(8,128)}) fusion(f32[4,512,3072]{2,1,0:T(8,128)} %fusion.204, f32[4,512]{1,0:T(4,128)S(1)} %dynamic-slice_bitcast_fusion.2, pred[512,3072]{1,0:T(8,128)(4,1)S(1)} %fusion.205, bf16[3072,4,80]{0,2,1:T(8,128)(2,1)} %get-tuple-element.627, ...), kind=kOutput, calls=%fused_computation.20.clone.1 | convolution fusion | flops 1031796736 | bytes 54214660 | tf_op jit(solution)/shard_map/while/body/eval_jaxpr/qhd,khd->hqk/dot_general | solution.py:138
  1013.7 21.8 %multiply_convert_fusion.8 = bf16[4,512,3072]{2,1,0:T(8,128)(2,1)} fusion(f32[4,512,3072]{2,1,0:T(8,128)} %get-tuple-element.550, f32[4,512,3072]{2,1,0:T(8,128)} %fusion.204, f32[4,512]{1,0:T(4,128)S(1)} %get-tuple-element.551, f32[4,512]{1,0:T(4,128)S(1)} %dynamic-slice_bitcast_fusion.2, pred[512,3072]{1,0:T(8,128)(4,1)S(1)} %fusion.205), kind=kLoop, calls=%fused_computation.19.clone.1 | loop fusion | flops 31457280 | bytes 64503808 | tf_op jit(solution)/shard_map/while/body/eval_jaxpr/convert_element_type | solution.py:142
  1169.6 121.9 %all-reduce.3.cloned.1.call-done = (f32[4,8,1280,16]{2,3,1,0:T(8,128)}, f32[4,8,16,1280]{3,2,1,0:T(8,128)}) async-done(((f32[4,8,1280,16]{2,3,1,0:T(8,128)}, f32[4,8,16,1280]{3,2,1,0:T(8,128)}), (f32[4,8,1280,16]{2,3,1,0:T(8,128)}, f32[4,8,16,1280]{3,2,1,0:T(8,128)})) %all-reduce.3.cloned.1.call-update) | async-done | bytes 5242896 | tf_op jit(solution)/shard_map/psum | solution.py:288
  (485 shorter events, 753.4 us)
Async XLA Ops:
  7.2 44.5 %all-gather.9.cloned.1.call-start = ((), (), s32[]{:S(2)}) async-start(), calls=%async_computation.9 | async-start | bytes 3686400 | tf_op jit(solution)/shard_map/all_gather | solution.py:203
  7.9 83.6 %all-gather.11.cloned.1.call-start = ((), (), s32[]{:S(2)}) async-start(), calls=%async_computation.10 | async-start | bytes 3686400 | tf_op jit(solution)/shard_map/all_gather | solution.py:204
  8.7 122.8 %all-gather.7.cloned.1.call-start = ((), (), s32[]{:S(2)}) async-start(), calls=%async_computation.8 | async-start | bytes 3686400 | tf_op jit(solution)/shard_map/all_gather | solution.py:202
  9.4 418.8 %all-gather.17.cloned.1.call-start = ((), (), s32[]{:S(2)}) async-start(), calls=%async_computation.13 | async-start | bytes 3686400 | tf_op jit(solution)/shard_map/all_gather | solution.py:207
  10.0 425.5 %all-gather.13.cloned.1.call-start = ((), (), s32[]{:S(2)}) async-start(), calls=%async_computation.11 | async-start | bytes 3686400 | tf_op jit(solution)/shard_map/all_gather | solution.py:205
  12.5 119.0 %copy-start.68 = (f32[768]{0:T(1024)}, f32[768]{0:T(1024)S(1)}, u32[]{:S(2)}) copy-start(f32[768]{0:T(1024)S(1)} %get-tuple-element.383) | copy-start | bytes 9220
  12.5 119.0 %copy-start.65 = (f32[1280]{0:T(1024)}, f32[1280]{0:T(1024)S(1)}, u32[]{:S(2)}) copy-start(f32[1280]{0:T(1024)S(1)} %convert_element_type.166) | copy-start | bytes 15364
  12.8 94.0 %copy-start.76 = (s32[768]{0:T(1024)}, s32[768]{0:T(1024)S(1)}, u32[]{:S(2)}) copy-start(s32[768]{0:T(1024)S(1)} %select_reduce_fusion.1) | copy-start | bytes 9220
  12.8 94.0 %copy-start.85 = (s32[128]{0:T(128)}, s32[128]{0:T(128)S(1)}, u32[]{:S(2)}) copy-start(s32[128]{0:T(128)S(1)} %and_select_fusion) | copy-start | bytes 1540
  15.1 42.6 %copy-start.30 = (bf16[1,1280,8,16]{1,3,2,0:T(8,128)(2,1)}, bf16[1,1280,8,16]{1,3,2,0:T(8,128)(2,1)S(1)}, u32[]{:S(2)}) copy-start(bf16[1,1280,8,16]{1,3,2,0:T(8,128)(2,1)S(1)} %get-tuple-element.378) | copy-start | bytes 983044
  15.1 91.7 %copy-start.39 = (bf16[1,1280,8,16]{1,3,2,0:T(8,128)(2,1)}, bf16[1,1280,8,16]{1,3,2,0:T(8,128)(2,1)S(1)}, u32[]{:S(2)}) copy-start(bf16[1,1280,8,16]{1,3,2,0:T(8,128)(2,1)S(1)} %get-tuple-element.379) | copy-start | bytes 983044
  15.9 80.4 %copy-start.43 = (bf16[768,128]{1,0:T(8,128)(2,1)}, bf16[768,128]{1,0:T(8,128)(2,1)S(1)}, u32[]{:S(2)}) copy-start(bf16[768,128]{1,0:T(8,128)(2,1)S(1)} %fusion.79) | copy-start | bytes 589828
  61.7 40.6 %all-to-all-start.1 = ((bf16[768,4,320]{0,2,1:T(8,128)(2,1)}), bf16[768,4,320]{0,2,1:T(8,128)(2,1)}, u32[]{:S(2)}, u32[]{:S(2)}) async-start(bf16[768,4,320]{0,2,1:T(8,128)(2,1)} %bitcast.294), calls=%async_computation.1 | async-start | bytes 3932160 | tf_op jit(solution)/shard_map/all_to_all | solution.py:219
  68.4 67.8 %copy-start.32 = (bf16[1,8,16,1280]{3,2,1,0:T(8,128)(2,1)}, bf16[1,8,16,1280]{3,2,1,0:T(8,128)(2,1)S(1)}, u32[]{:S(2)}) copy-start(bf16[1,8,16,1280]{3,2,1,0:T(8,128)(2,1)S(1)} %get-tuple-element.374) | copy-start | bytes 983044
  102.3 36.8 %all-to-all-start.2 = ((bf16[768,4,320]{0,2,1:T(8,128)(2,1)}), bf16[768,4,320]{0,2,1:T(8,128)(2,1)}, u32[]{:S(2)}, u32[]{:S(2)}) async-start(bf16[768,4,320]{0,2,1:T(8,128)(2,1)} %bitcast.293), calls=%async_computation.2 | async-start | bytes 3932160 | tf_op jit(solution)/shard_map/all_to_all | solution.py:220
  139.1 28.7 %all-to-all-start = ((bf16[768,4,320]{0,2,1:T(8,128)(2,1)}), bf16[768,4,320]{0,2,1:T(8,128)(2,1)}, u32[]{:S(2)}, u32[]{:S(2)}) async-start(bf16[768,4,320]{0,2,1:T(8,128)(2,1)} %bitcast.8), calls=%async_computation | async-start | bytes 3932160 | tf_op jit(solution)/shard_map/all_to_all | solution.py:218
  143.6 315.7 %all-gather.15.cloned.1.call-start = ((), (), s32[]{:S(2)}) async-start(), calls=%async_computation.12 | async-start | bytes 3686400 | tf_op jit(solution)/shard_map/all_gather | solution.py:206
  421.1 27.8 %all-to-all-start.3 = ((bf16[4,768,320]{1,2,0:T(8,128)(2,1)}), bf16[4,768,320]{1,2,0:T(8,128)(2,1)}, u32[]{:S(2)}, u32[]{:S(2)}) async-start(bf16[4,768,320]{1,2,0:T(8,128)(2,1)} %copy.80), calls=%async_computation.3 | async-start | bytes 3932160 | tf_op jit(solution)/shard_map/all_to_all | solution.py:223
  428.2 39.0 %copy-start.53 = (bf16[768,128]{1,0:T(8,128)(2,1)}, bf16[768,128]{1,0:T(8,128)(2,1)S(1)}, u32[]{:S(2)}) copy-start(bf16[768,128]{1,0:T(8,128)(2,1)S(1)} %fusion.85) | copy-start | bytes 589828
  486.4 27.5 %all-to-all-start.4 = ((bf16[4,768,320]{1,2,0:T(8,128)(2,1)}), bf16[4,768,320]{1,2,0:T(8,128)(2,1)}, u32[]{:S(2)}, u32[]{:S(2)}) async-start(bf16[4,768,320]{1,2,0:T(8,128)(2,1)} %copy.81), calls=%async_computation.4 | async-start | bytes 3932160 | tf_op jit(solution)/shard_map/all_to_all | solution.py:258
  1063.3 27.6 %all-to-all-start.7 = ((bf16[4,768,320]{1,2,0:T(8,128)(2,1)}), bf16[4,768,320]{1,2,0:T(8,128)(2,1)}, u32[]{:S(2)}, u32[]{:S(2)}) async-start(bf16[4,768,320]{1,2,0:T(8,128)(2,1)} %copy.89), calls=%async_computation.7 | async-start | bytes 3932160 | tf_op jit(solution)/shard_map/all_to_all | solution.py:269
  1090.9 26.7 %all-to-all-start.5 = ((bf16[4,768,320]{1,2,0:T(8,128)(2,1)}), bf16[4,768,320]{1,2,0:T(8,128)(2,1)S(1)}, u32[]{:S(2)}, u32[]{:S(2)}) async-start(bf16[4,768,320]{1,2,0:T(8,128)(2,1)} %copy.86), calls=%async_computation.5 | async-start | bytes 3932160 | tf_op jit(solution)/shard_map/all_to_all | solution.py:267
  1118.9 36.9 %all-to-all-start.6 = ((bf16[4,768,320]{1,2,0:T(8,128)(2,1)}), bf16[4,768,320]{1,2,0:T(8,128)(2,1)}, u32[]{:S(2)}, u32[]{:S(2)}) async-start(bf16[4,768,320]{1,2,0:T(8,128)(2,1)} %copy.88), calls=%async_computation.6 | async-start | bytes 3932160 | tf_op jit(solution)/shard_map/all_to_all | solution.py:268
  1123.4 168.1 %all-reduce.3.cloned.1.call-start = ((), (), s32[]{:S(2)}) async-start(), calls=%async_computation.14 | async-start | bytes 10485760 | tf_op jit(solution)/shard_map/psum | solution.py:288
  (125 other events, 877.6 us)
Sparse Core Ops, SparseCore 0:
  9.6 42.0 all-gather.8
  53.3 38.1 all-gather.10
  93.2 38.1 all-gather.6
  132.9 38.1 all-gather.16
  172.6 38.1 all-gather.12
  212.4 38.1 all-gather.14
  1143.8 147.6 all-reduce.2
